TPU v7x, 32 devices: a whole 2x2x4 slice. The times are simulated.
32 devices in a mesh: gx: 8 (over y, x, core), gy: 4 (over z).
Axes of the slice: x: 2, y: 2, z: 4, core: 2. Of those that a mesh axis runs over, the one named last changes fastest.
Arguments:
- state: bfloat16 [32, 12, 192, 256], P('gx', 'gy'), may hold values from -1 to 1
- weights: bfloat16 [32, 12, 9, 256, 256], P('gx', 'gy'), may hold values from -0.125 to 0.125
- drive: bfloat16 [2, 32, 12, 192, 256], P(None, 'gx', 'gy'), may hold values from -6 to 6
- leak: float32 [32, 12, 256], P('gx', 'gy'), may hold values from 0.1 to 1
- link_dev: int32 [8, 4, 12, 3], P(None, 'gy'), may hold values from 0 to 7, all different within a row; in each aligned block of 12 rows (0 to 11, 12 to 23, ..., all dimensions but the last counted through in order) at most 6 rows name the same one
- link_blk: int32 [8, 4, 12, 3], P(None, 'gy'), may hold values from 0 to 11
- offsets: int32 [5, 2], replicated, may hold values from -1 to 1, as said below
- gram_prev: float32 [32, 12, 256, 256], P('gx', 'gy'), may hold values from -6 to 6
Outputs:
- final_state: bfloat16 [32, 12, 192, 256], P('gx', 'gy')
- gram: float32 [32, 12, 256, 256], P('gx', 'gy')
Inputs may be any that keep to these rules, and one draw needn't show every extreme that they name: `link_dev`: the 3 sources of one block lie on different indices of gx; among the blocks of one device at most 6 sources lie on any one index of gx, and exactly 6 on some. Five distinct offsets.
All inputs are finite; a program needn't handle non-finite values.
Results may differ from a plain program's by a relative error of at most 0.0046.
Values may be sent and summed in bfloat16 or wider, within the bound.
A program may use at most 192 MiB of HBM per device.

v0:
```python
import functools

import jax
import jax.numpy as jnp
from jax import lax
from jax.experimental import pallas as pl
from jax.experimental.pallas import tpu as pltpu
from jax.sharding import PartitionSpec as P

MESH = pl.DeviceIdType.MESH
PART, ALONG_X, ALONG_Y, X_PART, Y_PART, DIAG, D_PART = range(7)


def padded(x, sides, width):
    for axis, dim in sides:
        size, length = (lax.axis_size(axis), x.shape[dim])
        up = [(i, (i + 1) % size) for i in range(size - 1)]
        down = [(j, i) for i, j in up]
        last = lax.slice_in_dim(x, length - width, length, axis=dim)
        first = lax.slice_in_dim(x, 0, width, axis=dim)
        before = lax.ppermute(last, axis, up)
        after = lax.ppermute(first, axis, down)
        x = jnp.concatenate([before, x, after], axis=dim)
    return x


def shards(state, weights, drive, leak, link_dev, link_blk, offsets, gram_prev):
    grid_rows, grid_cols, batch_cols, units = state.shape
    nblocks = grid_rows * grid_cols
    nlinks = link_dev.shape[-1]
    nstencil = offsets.shape[0]
    gx_size = lax.axis_size("gx")
    own_index = lax.axis_index("gx")
    all_dev = link_dev[:, 0].reshape(gx_size, nblocks * nlinks)
    all_blk = link_blk[:, 0].reshape(gx_size, nblocks * nlinks)
    my_dev = lax.dynamic_index_in_dim(all_dev, own_index, 0, keepdims=False)
    my_blk = lax.dynamic_index_in_dim(all_blk, own_index, 0, keepdims=False)
    w_long = weights[:, :, nstencil : nstencil + nlinks].reshape(nblocks, nlinks, units, units)
    current = state
    gram = gram_prev
    for step_id in range(drive.shape[0]):
        extended = padded(current, (("gx", 0), ("gy", 1)), 1)
        preact = jnp.zeros((grid_rows, grid_cols, batch_cols, units), jnp.float32)
        for offset_id in range(nstencil):
            zero = jnp.zeros((), jnp.int32)
            start_r = 1 + offsets[offset_id, 0]
            start_c = 1 + offsets[offset_id, 1]
            nearby = lax.dynamic_slice(
                extended, (start_r, start_c, zero, zero), (grid_rows, grid_cols, batch_cols, units)
            )
            preact = preact + jnp.einsum(
                "rcsu,rcuv->rcsv",
                nearby,
                weights[:, :, offset_id],
                preferred_element_type=jnp.float32,
            )
        flat_state = current.reshape(nblocks, batch_cols, units)
        whole = lax.all_gather(flat_state[None], "gx", axis=0, tiled=True)
        picked = whole.reshape(gx_size * nblocks, batch_cols, units)[my_dev * nblocks + my_blk]
        picked = picked.reshape(nblocks, nlinks, batch_cols, units)
        distant = jnp.einsum("blsu,bluv->bsv", picked, w_long, preferred_element_type=jnp.float32)
        preact = preact + distant.reshape(grid_rows, grid_cols, batch_cols, units)
        preact = preact + jnp.einsum(
            "rcsu,rcuv->rcsv",
            drive[step_id],
            weights[:, :, nstencil + nlinks],
            preferred_element_type=jnp.float32,
        )
        rate = leak[:, :, None, :]
        current = ((1.0 - rate) * current.astype(jnp.float32) + rate * jnp.tanh(preact)).astype(
            jnp.bfloat16
        )
        gram = gram + jnp.einsum(
            "rcsu,rcsv->rcuv", current, current, preferred_element_type=jnp.float32
        )
    return (current, gram)


def reservoir(
    n_gy, state, w, drive, leak, ldev, lblk, offs, gprev, out, gout,
    gath00, gath01, gath10, gath11, ext00, ext01, ext10, ext11, wv, dv, gv, acc, xf,
    load_sem, store_sem, send_sem, recv_sem, zsend_sem, zrecv_sem,
):
    rows, cols, seq, units = state.shape
    nstencil, nlinks = offs.shape[1], ldev.shape[1]
    half = seq // 2
    g, b = lax.axis_index("gx"), lax.axis_index("gy")
    core, x, y = lax.rem(g, 2), lax.rem(lax.div(g, 2), 2), lax.div(g, 4)
    near = lambda fy, fx, fc: (
        (1 - y if fy else y) * 4 + (1 - x if fx else x) * 2 + (1 - core if fc else core)
    )
    ids = {
        PART: near(0, 0, 1), ALONG_X: near(0, 1, 0), ALONG_Y: near(1, 0, 0),
        X_PART: near(0, 1, 1), Y_PART: near(1, 0, 1), DIAG: near(1, 1, 0), D_PART: near(1, 1, 1),
    }
    has_left, has_right = b > 0, b < n_gy - 1
    has_up, has_down = g > 0, g < 7
    gaths, exts = (gath00, gath01, gath10, gath11), (ext00, ext01, ext10, ext11)

    loads = []

    def load(src, dst):
        copy = pltpu.make_async_copy(src, dst, load_sem.at[len(loads)])
        copy.start()
        loads.append(copy)
        return copy

    for r in range(rows):
        for s in (0, 1):
            load(state.at[r, :, pl.ds(s * half, half)], gaths[s].at[g, pl.ds(r * cols, cols)])

    barrier = pltpu.get_barrier_semaphore()
    for rel in (PART, ALONG_X, ALONG_Y):
        pl.semaphore_signal(barrier, inc=1, device_id={"gx": ids[rel]}, device_id_type=MESH)

    @pl.when(has_left)
    def _():
        pl.semaphore_signal(barrier, inc=1, device_id={"gy": b - 1}, device_id_type=MESH)

    @pl.when(has_right)
    def _():
        pl.semaphore_signal(barrier, inc=1, device_id={"gy": b + 1}, device_id_type=MESH)

    inside = jnp.logical_and(has_left, has_right)

    @pl.when(inside)
    def _():
        pl.semaphore_wait(barrier, 5)

    @pl.when(jnp.logical_not(inside))
    def _():
        pl.semaphore_wait(barrier, 4 if n_gy > 1 else 3)

    sends = []

    def send(t, rel_from, r, to, rel_there):
        origin = g if rel_from is None else ids[rel_from]
        here = gaths[t].at[origin, pl.ds(r * cols, cols)]
        src = state.at[r, :, pl.ds(t * half, half)] if rel_from is None and t < 2 else here
        copy = pltpu.make_async_remote_copy(
            src_ref=src, dst_ref=here,
            send_sem=send_sem.at[len(sends)], recv_sem=recv_sem.at[t, rel_there, r],
            device_id={"gx": ids[to]}, device_id_type=MESH,
        )
        copy.start()
        sends.append(copy)

    def send_own(t, r, to):
        send(t, None, r, to, to)

    def arrived(t, rel, r):
        here = gaths[t].at[ids[rel], pl.ds(r * cols, cols)]
        pltpu.make_async_remote_copy(
            src_ref=here, dst_ref=here,
            send_sem=send_sem.at[0], recv_sem=recv_sem.at[t, rel, r],
            device_id={"gx": ids[PART]}, device_id_type=MESH,
        ).wait_recv()

    def relay(t, rel, r, across=None):
        arrived(t, rel, r)
        if across is not None:
            send(t, rel, r, across, DIAG)
        send(t, rel, r, PART, {ALONG_X: X_PART, ALONG_Y: Y_PART, DIAG: D_PART}[rel])

    def rim_copy(t, side, kind):
        col = 0 if side == 0 else cols - 1
        there = cols + 1 if side == 0 else 0
        gath, ext = gaths[t], exts[t]
        if kind == 0:
            return [
                pltpu.make_async_remote_copy(
                    src_ref=state.at[r, col, pl.ds(t * half, half)]
                    if t < 2
                    else gath.at[g, r * cols + col],
                    dst_ref=ext.at[r + 1, there],
                    send_sem=zsend_sem.at[t, side, r], recv_sem=zrecv_sem.at[t, side, r],
                    device_id={"gy": b - 1 if side == 0 else b + 1}, device_id_type=MESH,
                )
                for r in range(rows)
            ]
        src = (
            gath.at[lax.rem(g + 7, 8), (rows - 1) * cols + col]
            if kind == 1
            else gath.at[lax.rem(g + 1, 8), col]
        )
        return [
            pltpu.make_async_remote_copy(
                src_ref=src,
                dst_ref=ext.at[0 if kind == 1 else rows + 1, there],
                send_sem=zsend_sem.at[t, side, rows + kind - 1],
                recv_sem=zrecv_sem.at[t, side, rows + kind - 1],
                device_id={"gy": b - 1 if side == 0 else b + 1}, device_id_type=MESH,
            )
        ]

    def rims(t, do, kinds):
        for side in (0, 1):
            present = (has_left, has_right)
            who = present[side] if do != "wait_recv" else present[1 - side]
            for kind in kinds:
                cond = who
                if kind == 1:
                    cond = jnp.logical_and(who, has_up)
                if kind == 2:
                    cond = jnp.logical_and(who, has_down)

                @pl.when(cond)
                def _():
                    for copy in rim_copy(t, side, kind):
                        getattr(copy, do)()

    def begin(t, r):
        if r != 2:
            send_own(t, r, ALONG_X)
        if r != 1:
            send_own(t, r, ALONG_Y)
        send_own(t, r, PART)

    def exchange(t):
        relay(t, ALONG_X, 0, ALONG_Y)
        send_own(t, 1, ALONG_Y)
        relay(t, ALONG_Y, 0)
        relay(t, ALONG_X, 3)
        relay(t, ALONG_Y, 3, ALONG_X)
        send_own(t, 2, ALONG_X)
        relay(t, ALONG_X, 1, ALONG_Y)
        relay(t, ALONG_Y, 2, ALONG_X)

    def borders(t):
        relay(t, DIAG, 0)
        relay(t, DIAG, 3)
        for rel in (PART, X_PART, D_PART):
            arrived(t, rel, 0)
            arrived(t, rel, 3)
        rims(t, "start", (1, 2))
        fill(t)
        rims(t, "wait_recv", (0, 1, 2))

    def finish(t):
        relay(t, ALONG_Y, 1)
        relay(t, ALONG_X, 2)
        relay(t, DIAG, 1)
        relay(t, DIAG, 2)
        for rel in (PART, X_PART, D_PART):
            arrived(t, rel, 1)
            arrived(t, rel, 2)
        for r in range(rows):
            arrived(t, Y_PART, r)

    def fill(t):
        gath, ext = gaths[t], exts[t]

        def place(i, carry):
            r, c = i // cols, lax.rem(i, cols)
            ext[r + 1, c + 1] = gath[g, i]
            return carry

        lax.fori_loop(0, rows * cols, place, 0)
        zero = jnp.zeros((half, units), jnp.bfloat16)

        @pl.when(has_up)
        def _():
            for c in range(cols):
                ext[0, c + 1] = gath[lax.rem(g + 7, 8), (rows - 1) * cols + c]

        @pl.when(has_down)
        def _():
            for c in range(cols):
                ext[rows + 1, c + 1] = gath[lax.rem(g + 1, 8), c]

        for there, edge in ((0, has_up), (rows + 1, has_down)):

            @pl.when(jnp.logical_not(edge))
            def _():
                for c in range(cols + 2):
                    ext[there, c] = zero

        for there, side in ((0, has_left), (cols + 1, has_right)):

            @pl.when(jnp.logical_not(side))
            def _():
                for r in range(rows):
                    ext[r + 1, there] = zero
                for r, edge in ((0, has_up), (rows + 1, has_down)):

                    @pl.when(edge)
                    def _():
                        ext[r, there] = zero

    def dot(a, weight):
        return jnp.dot(a, weight, preferred_element_type=jnp.float32)

    def nearby(t):
        ext = exts[t]

        def one(i, carry):
            r, c = i // cols, lax.rem(i, cols)
            total = dot(
                dv[t // 2, r, c, pl.ds(t % 2 * half, half)], wv[r, c, nstencil + nlinks]
            )
            for k in range(nstencil):
                total = total + dot(ext[r + 1 + offs[0, k], c + 1 + offs[1, k]], wv[r, c, k])
            acc[i] = total
            return carry

        lax.fori_loop(0, rows * cols, one, 0)

    def gram_of(r, c, now):
        gv[r, c] += lax.dot_general(
            now, now, (((0,), (0,)), ((), ())), preferred_element_type=jnp.float32
        )

    def distant(t, r):
        gath = gaths[t]

        def one(c, carry):
            i = r * cols + c
            total = acc[i]
            for l in range(nlinks):
                total = total + dot(gath[ldev[g, l, 0, i], lblk[g, l, 0, i]], wv[r, c, nstencil + l])
            rate = leak[c, pl.ds(r, 1), :]
            old = gath[g, i].astype(jnp.float32)
            now = ((1.0 - rate) * old + rate * jnp.tanh(total)).astype(jnp.bfloat16)
            if t >= 2:
                xf[i, pl.ds((t - 2) * half, half)] = now
            else:
                gaths[t + 2][g, i] = now
                gram_of(r, c, now)
            return carry

        lax.fori_loop(0, cols, one, 0)

    order = (0, 3, 1, 2)

    def start(t):
        for r in order:
            begin(t, r)
        rims(t, "start", (0,))

    stores = []

    def store(src, dst):
        copy = pltpu.make_async_copy(src, dst, store_sem.at[len(stores)])
        copy.start()
        stores.append(copy)

    start(0)
    for r in range(rows):
        load(w.at[r], wv.at[r])
    load(drive, dv)
    load(gprev, gv)
    for t in range(4):
        exchange(t)
        if t < 3:
            start(t + 1)
        if t == 0:
            for copy in loads:
                copy.wait()
        borders(t)
        nearby(t)
        finish(t)
        for r in range(rows):
            distant(t, r)
            if t == 3:
                store(xf.at[pl.ds(r * cols, cols)], out.at[r])
        if t == 1:
            store(gv, gout)
    for copy in sends:
        copy.wait_send()
    for t in range(4):
        rims(t, "wait_send", (0, 1, 2))
    for copy in stores:
        copy.wait()


def closing(x, gram, out, gout, xv, gv, x_sem, g_sem, out_sem, gout_sem):
    rows, cols = x.shape[:2]
    copy = pltpu.make_async_copy
    x_in = [copy(x.at[r], xv.at[r], x_sem.at[r]) for r in range(rows)]
    g_in = [copy(gram.at[r], gv.at[r], g_sem.at[r]) for r in range(rows)]
    x_out = [copy(xv.at[r], out.at[r], out_sem.at[r]) for r in range(rows)]
    g_out = [copy(gv.at[r], gout.at[r], gout_sem.at[r]) for r in range(rows)]
    for r in range(rows):
        x_in[r].start()
        g_in[r].start()
    for r in range(rows):
        x_in[r].wait()
        x_out[r].start()
        g_in[r].wait()
        for c in range(cols):
            now = xv[r, c]
            gv[r, c] += lax.dot_general(
                now, now, (((0,), (0,)), ((), ())), preferred_element_type=jnp.float32
            )
        g_out[r].start()
    for r in range(rows):
        x_out[r].wait()
        g_out[r].wait()


def fast_shards(n_gy, state, weights, drive, leak, link_dev, link_blk, offsets, gram_prev):
    rows, cols, seq, units = state.shape
    blocks = rows * cols
    anywhere = pl.BlockSpec(memory_space=pl.ANY)
    scalars = pl.BlockSpec(memory_space=pltpu.SMEM)
    block = (seq // 2, units)
    last, gram = pl.pallas_call(
        functools.partial(reservoir, n_gy),
        out_shape=(
            jax.ShapeDtypeStruct(state.shape, state.dtype),
            jax.ShapeDtypeStruct(gram_prev.shape, gram_prev.dtype),
        ),
        in_specs=[
            anywhere, anywhere, anywhere, pl.BlockSpec(memory_space=pltpu.VMEM),
            scalars, scalars, scalars, anywhere,
        ],
        out_specs=(anywhere, anywhere),
        scratch_shapes=[
            *[pltpu.VMEM((8, blocks, *block), jnp.bfloat16)] * 4,
            *[pltpu.VMEM((rows + 2, cols + 2, *block), jnp.bfloat16)] * 4,
            pltpu.VMEM(weights.shape, weights.dtype),
            pltpu.VMEM(drive.shape, drive.dtype),
            pltpu.VMEM(gram_prev.shape, gram_prev.dtype),
            pltpu.VMEM((blocks, *block), jnp.float32),
            pltpu.VMEM((blocks, seq, units), jnp.bfloat16),
            pltpu.SemaphoreType.DMA((14,)),
            pltpu.SemaphoreType.DMA((8,)),
            pltpu.SemaphoreType.DMA((112,)),
            pltpu.SemaphoreType.DMA((4, 7, 4)),
            pltpu.SemaphoreType.DMA((4, 2, 6)),
            pltpu.SemaphoreType.DMA((4, 2, 6)),
        ],
        compiler_params=pltpu.CompilerParams(
            collective_id=0, has_side_effects=True, vmem_limit_bytes=62 * 1024 * 1024
        ),
    )(
        state, weights, drive, leak.transpose(1, 0, 2), link_dev.transpose(0, 3, 1, 2),
        link_blk.transpose(0, 3, 1, 2), offsets.T, gram_prev,
    )
    return pl.pallas_call(
        closing,
        out_shape=(
            jax.ShapeDtypeStruct(state.shape, state.dtype),
            jax.ShapeDtypeStruct(gram_prev.shape, gram_prev.dtype),
        ),
        in_specs=[anywhere, anywhere],
        out_specs=(anywhere, anywhere),
        scratch_shapes=[
            pltpu.VMEM(state.shape, state.dtype),
            pltpu.VMEM(gram_prev.shape, gram_prev.dtype),
            *[pltpu.SemaphoreType.DMA((rows,))] * 4,
        ],
        compiler_params=pltpu.CompilerParams(vmem_limit_bytes=62 * 1024 * 1024),
    )(last, gram)


def solution(mesh):
    part = shards
    if mesh.shape["gx"] == 8:
        part = functools.partial(fast_shards, mesh.shape["gy"])
    return jax.shard_map(
        part,
        mesh=mesh,
        in_specs=(
            P("gx", "gy", None, None),
            P("gx", "gy", None, None, None),
            P(None, "gx", "gy", None, None),
            P("gx", "gy", None),
            P(None, "gy", None, None),
            P(None, "gy", None, None),
            P(),
            P("gx", "gy", None, None),
        ),
        out_specs=(P("gx", "gy", None, None), P("gx", "gy", None, None)),
        check_vma=False,
    )
```

profile of v0, /device:TPU:0, one launch (start us, length us, event | category | flops | bytes accessed | tf_op | source)
XLA Modules:
  0.0 102.5 jit_solution(13635488082321581025)
XLA Ops:
  0.6 98.2 %shard_map.95 = (bf16[4,3,192,256]{3,2,1,0:T(8,128)(2,1)}, f32[4,3,256,256]{3,2,1,0:T(8,128)}) custom-call(bf16[4,3,192,256]{3,2,1,0:T(8,128)(2,1)} %state.1, bf16[4,3,9,256,256]{4,3,2,1,0:T(8,128)(2,1)} %w.1, bf16[2,4,3,192,256]{4,3,2,1,0:T(8,128)(2,1)} %drive.1, f32[3,4,256]{2,1,0:T(4,128)} %bitcast.4, s32[8,3,1,12]{3,2,1,0:T(1,128)} %bitcast.5, ...), custom_call_target="tpu_custom_call" | custom-call | tf_op jit(solution)/shard_map/pallas_call | solution.py:407
  98.9 3.6 %shard_map.96 = (bf16[4,3,192,256]{3,2,1,0:T(8,128)(2,1)}, f32[4,3,256,256]{3,2,1,0:T(8,128)}) custom-call(bf16[4,3,192,256]{3,2,1,0:T(8,128)(2,1)} %get-tuple-element.4.x, f32[4,3,256,256]{3,2,1,0:T(8,128)} %get-tuple-element.5.gram), custom_call_target="tpu_custom_call" | custom-call | tf_op jit(solution)/shard_map/pallas_call | solution.py:440
where the time goes:
time: 103 us
  Pallas kernels  102 us (99%)
    pallas_call x1, Pallas kernels, fast_shards(): pl.pallas_call(functools.partial(reservoir, n_gy), out_shape=(jax.ShapeDt...  98.2 us
    pallas_call x1, Pallas kernels, fast_shards(): pl.pallas_call(closing, out_shape=(jax.ShapeDtypeStruct(state.shape, stat...  3.65 us

commit v1 on v0

--- a/solution.py
+++ b/solution.py
@@ -77,13 +77,16 @@
 
 
 def reservoir(
-    n_gy, state, w, drive, leak, ldev, lblk, offs, gprev, out, gout,
-    gath00, gath01, gath10, gath11, ext00, ext01, ext10, ext11, wv, dv, gv, acc, xf,
-    load_sem, store_sem, send_sem, recv_sem, zsend_sem, zrecv_sem,
+    n_gy, sizes, state, w, drive, leak, ldev, lblk, offs, gprev, out, gout, *scratch
 ):
+    parts = len(sizes)
+    phases = drive.shape[0] * parts
+    last = phases - 1
+    gaths, exts, rest = scratch[:phases], scratch[phases : 2 * phases], scratch[2 * phases :]
+    wv, dv, gv, acc, xf, load_sem, store_sem, send_sem, recv_sem, zsend_sem, zrecv_sem = rest
     rows, cols, seq, units = state.shape
     nstencil, nlinks = offs.shape[1], ldev.shape[1]
-    half = seq // 2
+    spans = [pl.ds(sum(sizes[: t % parts]), sizes[t % parts]) for t in range(phases)]
     g, b = lax.axis_index("gx"), lax.axis_index("gy")
     core, x, y = lax.rem(g, 2), lax.rem(lax.div(g, 2), 2), lax.div(g, 4)
     near = lambda fy, fx, fc: (
@@ -95,7 +98,6 @@
     }
     has_left, has_right = b > 0, b < n_gy - 1
     has_up, has_down = g > 0, g < 7
-    gaths, exts = (gath00, gath01, gath10, gath11), (ext00, ext01, ext10, ext11)
 
     loads = []
 
@@ -106,8 +108,8 @@
         return copy
 
     for r in range(rows):
-        for s in (0, 1):
-            load(state.at[r, :, pl.ds(s * half, half)], gaths[s].at[g, pl.ds(r * cols, cols)])
+        for s in range(parts):
+            load(state.at[r, :, spans[s]], gaths[s].at[g, pl.ds(r * cols, cols)])
 
     barrier = pltpu.get_barrier_semaphore()
     for rel in (PART, ALONG_X, ALONG_Y):
@@ -136,7 +138,7 @@
     def send(t, rel_from, r, to, rel_there):
         origin = g if rel_from is None else ids[rel_from]
         here = gaths[t].at[origin, pl.ds(r * cols, cols)]
-        src = state.at[r, :, pl.ds(t * half, half)] if rel_from is None and t < 2 else here
+        src = state.at[r, :, spans[t]] if rel_from is None and t < parts else here
         copy = pltpu.make_async_remote_copy(
             src_ref=src, dst_ref=here,
             send_sem=send_sem.at[len(sends)], recv_sem=recv_sem.at[t, rel_there, r],
@@ -169,8 +171,8 @@
         if kind == 0:
             return [
                 pltpu.make_async_remote_copy(
-                    src_ref=state.at[r, col, pl.ds(t * half, half)]
-                    if t < 2
+                    src_ref=state.at[r, col, spans[t]]
+                    if t < parts
                     else gath.at[g, r * cols + col],
                     dst_ref=ext.at[r + 1, there],
                     send_sem=zsend_sem.at[t, side, r], recv_sem=zrecv_sem.at[t, side, r],
@@ -209,20 +211,25 @@
                     for copy in rim_copy(t, side, kind):
                         getattr(copy, do)()
 
-    def begin(t, r):
-        if r != 2:
-            send_own(t, r, ALONG_X)
-        if r != 1:
-            send_own(t, r, ALONG_Y)
-        send_own(t, r, PART)
+    def upfront(t):
+        return 3 if t == last else 4
+
+    def start(t):
+        for x_row, y_row in ((0, 3), (3, 0), (1, 2), (2, 1))[: upfront(t)]:
+            send_own(t, x_row, ALONG_X)
+            send_own(t, y_row, ALONG_Y)
+            send_own(t, x_row, PART)
+        rims(t, "start", (0,))
 
     def exchange(t):
         relay(t, ALONG_X, 0, ALONG_Y)
-        send_own(t, 1, ALONG_Y)
+        relay(t, ALONG_Y, 3, ALONG_X)
+        for x_row, y_row in ((0, 3), (3, 0), (1, 2), (2, 1))[upfront(t) :]:
+            send_own(t, x_row, ALONG_X)
+            send_own(t, y_row, ALONG_Y)
+            send_own(t, x_row, PART)
         relay(t, ALONG_Y, 0)
         relay(t, ALONG_X, 3)
-        relay(t, ALONG_Y, 3, ALONG_X)
-        send_own(t, 2, ALONG_X)
         relay(t, ALONG_X, 1, ALONG_Y)
         relay(t, ALONG_Y, 2, ALONG_X)
 
@@ -256,7 +263,7 @@
             return carry
 
         lax.fori_loop(0, rows * cols, place, 0)
-        zero = jnp.zeros((half, units), jnp.bfloat16)
+        zero = jnp.zeros((sizes[t % parts], units), jnp.bfloat16)
 
         @pl.when(has_up)
         def _():
@@ -295,15 +302,13 @@
 
         def one(i, carry):
             r, c = i // cols, lax.rem(i, cols)
-            total = dot(
-                dv[t // 2, r, c, pl.ds(t % 2 * half, half)], wv[r, c, nstencil + nlinks]
-            )
+            total = dot(dv[t // parts, r, c, spans[t]], wv[r, c, nstencil + nlinks])
             for k in range(nstencil):
                 total = total + dot(ext[r + 1 + offs[0, k], c + 1 + offs[1, k]], wv[r, c, k])
-            acc[i] = total
+            acc[i, pl.ds(0, sizes[t % parts])] = total
             return carry
 
-        lax.fori_loop(0, rows * cols, one, 0)
+        lax.fori_loop(0, rows * cols, one, 0, unroll=True)
 
     def gram_of(r, c, now):
         gv[r, c] += lax.dot_general(
@@ -315,27 +320,20 @@
 
         def one(c, carry):
             i = r * cols + c
-            total = acc[i]
+            total = acc[i, pl.ds(0, sizes[t % parts])]
             for l in range(nlinks):
                 total = total + dot(gath[ldev[g, l, 0, i], lblk[g, l, 0, i]], wv[r, c, nstencil + l])
             rate = leak[c, pl.ds(r, 1), :]
             old = gath[g, i].astype(jnp.float32)
             now = ((1.0 - rate) * old + rate * jnp.tanh(total)).astype(jnp.bfloat16)
-            if t >= 2:
-                xf[i, pl.ds((t - 2) * half, half)] = now
+            if t + parts >= phases:
+                xf[i, spans[t]] = now
             else:
-                gaths[t + 2][g, i] = now
+                gaths[t + parts][g, i] = now
                 gram_of(r, c, now)
             return carry
 
-        lax.fori_loop(0, cols, one, 0)
-
-    order = (0, 3, 1, 2)
-
-    def start(t):
-        for r in order:
-            begin(t, r)
-        rims(t, "start", (0,))
+        lax.fori_loop(0, cols, one, 0, unroll=True)
 
     stores = []
 
@@ -349,9 +347,9 @@
         load(w.at[r], wv.at[r])
     load(drive, dv)
     load(gprev, gv)
-    for t in range(4):
+    for t in range(phases):
         exchange(t)
-        if t < 3:
+        if t < last:
             start(t + 1)
         if t == 0:
             for copy in loads:
@@ -361,13 +359,13 @@
         finish(t)
         for r in range(rows):
             distant(t, r)
-            if t == 3:
+            if t == last:
                 store(xf.at[pl.ds(r * cols, cols)], out.at[r])
-        if t == 1:
+        if t == phases - parts - 1:
             store(gv, gout)
     for copy in sends:
         copy.wait_send()
-    for t in range(4):
+    for t in range(phases):
         rims(t, "wait_send", (0, 1, 2))
     for copy in stores:
         copy.wait()
@@ -401,11 +399,13 @@
 def fast_shards(n_gy, state, weights, drive, leak, link_dev, link_blk, offsets, gram_prev):
     rows, cols, seq, units = state.shape
     blocks = rows * cols
+    steps = drive.shape[0]
+    sizes = (96, 96)
+    parts, phases = len(sizes), steps * len(sizes)
     anywhere = pl.BlockSpec(memory_space=pl.ANY)
     scalars = pl.BlockSpec(memory_space=pltpu.SMEM)
-    block = (seq // 2, units)
     last, gram = pl.pallas_call(
-        functools.partial(reservoir, n_gy),
+        functools.partial(reservoir, n_gy, sizes),
         out_shape=(
             jax.ShapeDtypeStruct(state.shape, state.dtype),
             jax.ShapeDtypeStruct(gram_prev.shape, gram_prev.dtype),
@@ -416,19 +416,19 @@
         ],
         out_specs=(anywhere, anywhere),
         scratch_shapes=[
-            *[pltpu.VMEM((8, blocks, *block), jnp.bfloat16)] * 4,
-            *[pltpu.VMEM((rows + 2, cols + 2, *block), jnp.bfloat16)] * 4,
+            *[pltpu.VMEM((8, blocks, m, units), jnp.bfloat16) for m in sizes] * steps,
+            *[pltpu.VMEM((rows + 2, cols + 2, m, units), jnp.bfloat16) for m in sizes] * steps,
             pltpu.VMEM(weights.shape, weights.dtype),
             pltpu.VMEM(drive.shape, drive.dtype),
             pltpu.VMEM(gram_prev.shape, gram_prev.dtype),
-            pltpu.VMEM((blocks, *block), jnp.float32),
+            pltpu.VMEM((blocks, max(sizes), units), jnp.float32),
             pltpu.VMEM((blocks, seq, units), jnp.bfloat16),
-            pltpu.SemaphoreType.DMA((14,)),
-            pltpu.SemaphoreType.DMA((8,)),
-            pltpu.SemaphoreType.DMA((112,)),
-            pltpu.SemaphoreType.DMA((4, 7, 4)),
-            pltpu.SemaphoreType.DMA((4, 2, 6)),
-            pltpu.SemaphoreType.DMA((4, 2, 6)),
+            pltpu.SemaphoreType.DMA((rows * (parts + 1) + 2,)),
+            pltpu.SemaphoreType.DMA((2 * rows,)),
+            pltpu.SemaphoreType.DMA((28 * phases,)),
+            pltpu.SemaphoreType.DMA((phases, 7, rows)),
+            pltpu.SemaphoreType.DMA((phases, 2, rows + 2)),
+            pltpu.SemaphoreType.DMA((phases, 2, rows + 2)),
         ],
         compiler_params=pltpu.CompilerParams(
             collective_id=0, has_side_effects=True, vmem_limit_bytes=62 * 1024 * 1024

time: 103 us -> 94.3 us (0.916)
  Pallas kernels: 102 us -> 93.3 us
    pallas_call x1, Pallas kernels: 98.2 us -> 89.6 us  [fast_shards(): pl.pallas_call(functools.partial(reservoir, n_gy, sizes), out_shape=(jax....]
where the time goes in v1:
time: 94.3 us; the launch traced here: 94.1 us
  Pallas kernels  93.3 us (99%)
    pallas_call x1, Pallas kernels, fast_shards(): pl.pallas_call(functools.partial(reservoir, n_gy, sizes), out_shape=(jax....  89.6 us
    pallas_call x1, Pallas kernels, fast_shards(): pl.pallas_call(closing, out_shape=(jax.ShapeDtypeStruct(state.shape, stat...  3.65 us

profile of v1, /device:TPU:0, one launch (start us, length us, event | category | flops | bytes accessed | tf_op | source)
XLA Modules:
  0.0 94.1 jit_solution(10428385398521021060)
XLA Ops:
  0.6 89.6 %shard_map.95 = (bf16[4,3,192,256]{3,2,1,0:T(8,128)(2,1)}, f32[4,3,256,256]{3,2,1,0:T(8,128)}) custom-call(bf16[4,3,192,256]{3,2,1,0:T(8,128)(2,1)} %state.1, bf16[4,3,9,256,256]{4,3,2,1,0:T(8,128)(2,1)} %w.1, bf16[2,4,3,192,256]{4,3,2,1,0:T(8,128)(2,1)} %drive.1, f32[3,4,256]{2,1,0:T(4,128)} %bitcast.4, s32[8,3,1,12]{3,2,1,0:T(1,128)} %bitcast.5, ...), custom_call_target="tpu_custom_call" | custom-call | tf_op jit(solution)/shard_map/pallas_call | solution.py:407
  90.3 3.6 %shard_map.96 = (bf16[4,3,192,256]{3,2,1,0:T(8,128)(2,1)}, f32[4,3,256,256]{3,2,1,0:T(8,128)}) custom-call(bf16[4,3,192,256]{3,2,1,0:T(8,128)(2,1)} %get-tuple-element.4.x, f32[4,3,256,256]{3,2,1,0:T(8,128)} %get-tuple-element.5.gram), custom_call_target="tpu_custom_call" | custom-call | tf_op jit(solution)/shard_map/pallas_call | solution.py:440
